TPU v7x, 128 devices: a whole 4x4x4 slice. The times are simulated.
128 devices in a mesh: row: 8 (over z, x_hi), col: 16 (over y, x_lo, core).
Axes of the slice: x: 4 (x_hi: 2, x_lo: 2; x = x_hi * 2 + x_lo), y: 4, z: 4, core: 2. Of those that a mesh axis runs over, the one named last changes fastest.
Arguments:
- features: bfloat16 [32768, 512], P('row'), may hold values from -6 to 6
- logits: float32 [32768, 128], P(('row', 'col')), may hold values from -16 to 16
Outputs:
- memberships: float32 [32768, 128], P(('row', 'col'))
- standardized: float32 [32768, 128], P(('row', 'col'))
All inputs are finite; a program needn't handle non-finite values.
Results may differ from a plain program's by a relative error of at most 0.0003.
Values may be sent and summed in bfloat16 or wider, within the bound.
A program may use at most 64 MiB of HBM per device.

v0:
```python
import math
import jax
import jax.numpy as jnp
from jax import lax
from jax.sharding import PartitionSpec as P

ITERS = 2


def kernel_product(left_rows, right_rows, members):
    count = left_rows.shape[0]
    feature_width = left_rows.shape[1]
    block_rows = math.gcd(count, 512)
    blocks = left_rows.reshape(count // block_rows, block_rows, feature_width)

    def block_product(block):
        inner = jnp.einsum("bf,nf->bn", block, right_rows, preferred_element_type=jnp.float32)
        base = 1.0 + inner / feature_width
        kernel = base * base * base
        return jnp.dot(
            kernel, members, precision=lax.Precision.HIGHEST, preferred_element_type=jnp.float32
        )

    return lax.map(block_product, blocks).reshape(count, members.shape[1])


def on_device(features, logits):
    frames = logits.shape[0]
    column = lax.axis_index("col")
    own_rows = lax.dynamic_slice_in_dim(features, column * frames, frames, 0)
    column_panel = lax.all_gather(own_rows, "row", axis=0, tiled=True)
    raised = jnp.exp(logits)
    members = raised / jnp.sum(raised, axis=1, keepdims=True)
    standardized = members
    for iteration in range(ITERS):
        members_column = lax.all_gather(members, "row", axis=0, tiled=True)
        scores = lax.psum_scatter(
            kernel_product(features, column_panel, members_column),
            "col",
            scatter_dimension=0,
            tiled=True,
        )
        cluster_size, weighted = lax.psum(
            (jnp.sum(members, axis=0), jnp.sum(members * scores, axis=0)), ("row", "col")
        )
        compact = weighted / (cluster_size * cluster_size)
        distance = compact[None, :] - 2.0 * scores / cluster_size[None, :]
        centered = distance - jnp.mean(distance, axis=1, keepdims=True)
        spread = jnp.mean(centered * centered, axis=1, keepdims=True)
        standardized = centered / jnp.sqrt(spread + 1e-06)
        raised = jnp.exp(-2.0 * standardized)
        members = raised / jnp.sum(raised, axis=1, keepdims=True)
    return (members, standardized)


def solution(mesh):
    return jax.shard_map(
        on_device,
        mesh=mesh,
        in_specs=(P("row", None), P(("row", "col"), None)),
        out_specs=(P(("row", "col"), None), P(("row", "col"), None)),
        check_vma=False,
    )
```

profile of v0, /device:TPU:1, one launch (start us, length us, event | category | flops | bytes accessed | tf_op | source)
XLA Modules:
  0.0 545.2 jit_solution(2299477837792060629)
XLA Ops:
  8.2 1.7 exponential_divide_fusion
  10.0 1.7 constant_dynamic-slice_fusion
  11.7 47.2 %all-gather.6.cloned.1.call-done = f32[2048,128]{1,0:T(8,128)} async-done(((f32[256,128]{1,0:T(8,128)}), f32[2048,128]{1,0:T(8,128)}) %all-gather.6.cloned.1.call-update) | async-done | bytes 1048592 | tf_op jit(solution)/shard_map/all_gather | solution.py:36
  59.0 55.7 %all-gather.4.cloned.1.call-done = bf16[2048,512]{1,0:T(8,128)(2,1)} async-done(((bf16[256,512]{1,0:T(8,128)(2,1)}), bf16[2048,512]{1,0:T(8,128)(2,1)}) %all-gather.4.cloned.1.call-update) | async-done | bytes 2097168 | tf_op jit(solution)/shard_map/all_gather | solution.py:31
  114.8 54.8 %while.20 = (s32[]{:T(128)}, f32[8,512,128]{2,1,0:T(8,128)S(1)}, bf16[8,512,512]{2,1,0:T(8,128)(2,1)}, bf16[2048,512]{1,0:T(8,128)(2,1)}, f32[2048,128]{1,0:T(8,128)}, /*index=5*/s32[]{:T(128)}) while((s32[]{:T(128)}, f32[8,512,128]{2,1,0:T(8,128)S(1)}, bf16[8,512,512]{2,1,0:T(8,128)(2,1)}, bf16[2048,512]{1,0:T(8,128)(2,1)}, ...), condition=%wide.region_2.3_spmd, body=%wide.region_1.2_spmd.sunk | while | flops 2688548864 | bytes 16515685 | solution.py:24
  114.9 3.1 fusion.48
  118.0 3.7 fusion.49
  121.7 3.1 fusion.48
  124.9 3.7 fusion.49
  128.6 3.1 fusion.48
  131.7 3.7 fusion.49
  135.4 3.1 fusion.48
  138.6 3.7 fusion.49
  142.3 3.1 fusion.48
  145.4 3.7 fusion.49
  149.1 3.1 fusion.48
  152.3 3.7 fusion.49
  156.0 3.1 fusion.48
  159.1 3.7 fusion.49
  162.8 3.1 fusion.48
  166.0 3.7 fusion.49
  169.7 1.3 copy-done.1
  171.0 60.5 %reduce-scatter.3.cloned.1.call-done = f32[256,128]{1,0:T(8,128)} async-done(((f32[4096,128]{1,0:T(8,128)}), f32[256,128]{1,0:T(8,128)}) %reduce-scatter.3.cloned.1.call-update) | async-done | bytes 131088 | tf_op jit(solution)/shard_map/reduce_scatter | solution.py:37
  232.5 68.0 %all-reduce.1 = (f32[128]{0:T(128)S(1)}, f32[128]{0:T(128)S(1)}) all-reduce(f32[128]{0:T(128)S(1)} %get-tuple-element.61, f32[128]{0:T(128)S(1)} %get-tuple-element.60), channel_id=1, replica_groups=mesh['row'=8,'col'=16] {'row','col'}, use_global_device_ids=true, to_apply=%region_7.8 | all-reduce | flops 256 | bytes 2048 | tf_op jit(solution)/shard_map/psum | solution.py:43
  302.7 1.1 fusion.28
  303.8 1.7 broadcast_divide_fusion
  305.8 41.2 %all-gather.8.cloned.1.call-done = f32[2048,128]{1,0:T(8,128)} async-done(((f32[256,128]{1,0:T(8,128)}), f32[2048,128]{1,0:T(8,128)}) %all-gather.8.cloned.1.call-update) | async-done | bytes 1048592 | tf_op jit(solution)/shard_map/all_gather | solution.py:36
  347.2 54.8 %while.21 = (s32[]{:T(128)}, f32[8,512,128]{2,1,0:T(8,128)S(1)}, bf16[8,512,512]{2,1,0:T(8,128)(2,1)}, bf16[2048,512]{1,0:T(8,128)(2,1)}, f32[2048,128]{1,0:T(8,128)}, /*index=5*/s32[]{:T(128)}) while((s32[]{:T(128)}, f32[8,512,128]{2,1,0:T(8,128)S(1)}, bf16[8,512,512]{2,1,0:T(8,128)(2,1)}, bf16[2048,512]{1,0:T(8,128)(2,1)}, ...), condition=%wide.region_12.13_spmd, body=%wide.region_11.12_spmd.sunk | while | flops 2688548864 | bytes 16515685 | solution.py:24
  347.2 3.1 fusion.53
  350.3 3.7 fusion.54
  354.1 3.1 fusion.53
  357.2 3.7 fusion.54
  360.9 3.1 fusion.53
  364.1 3.7 fusion.54
  367.8 3.1 fusion.53
  370.9 3.7 fusion.54
  374.6 3.1 fusion.53
  377.8 3.7 fusion.54
  381.5 3.1 fusion.53
  384.6 3.7 fusion.54
  388.3 3.1 fusion.53
  391.5 3.7 fusion.54
  395.2 3.1 fusion.53
  398.3 3.7 fusion.54
  402.0 1.3 copy-done
  403.4 62.6 %reduce-scatter.5.cloned.1.call-done = f32[256,128]{1,0:T(8,128)} async-done(((f32[4096,128]{1,0:T(8,128)}), f32[256,128]{1,0:T(8,128)}) %reduce-scatter.5.cloned.1.call-update) | async-done | bytes 131088 | tf_op jit(solution)/shard_map/reduce_scatter | solution.py:37
  467.1 67.5 %all-reduce = (f32[128]{0:T(128)S(1)}, f32[128]{0:T(128)S(1)}) all-reduce(f32[128]{0:T(128)S(1)} %get-tuple-element.59, f32[128]{0:T(128)S(1)} %get-tuple-element.58), channel_id=1, replica_groups=mesh['row'=8,'col'=16] {'row','col'}, use_global_device_ids=true, to_apply=%region_17.18 | all-reduce | flops 256 | bytes 2048 | tf_op jit(solution)/shard_map/psum | solution.py:43
  536.7 1.1 fusion.27
  (66 shorter events, 9.0 us)
Async XLA Ops:
  7.2 51.8 %all-gather.6.cloned.1.call-start = ((), (), s32[]{:S(2)}) async-start(), calls=%async_computation.3 | async-start | bytes 1179648 | tf_op jit(solution)/shard_map/all_gather | solution.py:36
  9.9 104.8 %all-gather.4.cloned.1.call-start = ((), (), s32[]{:S(2)}) async-start(), calls=%async_computation.2 | async-start | bytes 2359296 | tf_op jit(solution)/shard_map/all_gather | solution.py:31
  11.7 219.8 %reduce-scatter.3.cloned.1.call-start = ((), (), s32[]{:S(2)}) async-start(), calls=%async_computation.4 | async-start | bytes 2228224 | tf_op jit(solution)/shard_map/reduce_scatter | solution.py:37
  114.8 116.7 %copy-start.3 = (f32[256,128]{1,0:T(8,128)S(1)}, f32[256,128]{1,0:T(8,128)}, u32[]{:S(2)}) copy-start(f32[256,128]{1,0:T(8,128)} %param.7) | copy-start | bytes 393220
  114.8 3.1 copy-start.5
  121.7 3.1 copy-start.5
  128.6 3.1 copy-start.5
  135.4 3.1 copy-start.5
  142.3 3.1 copy-start.5
  149.1 3.1 copy-start.5
  156.0 3.1 copy-start.5
  162.8 3.1 copy-start.5
  169.7 1.3 copy-start.1
  171.0 176.0 %all-gather.8.cloned.1.call-start = ((), (), s32[]{:S(2)}) async-start(), calls=%async_computation.5 | async-start | bytes 1179648 | tf_op jit(solution)/shard_map/all_gather | solution.py:36
  305.6 160.4 %reduce-scatter.5.cloned.1.call-start = ((), (), s32[]{:S(2)}) async-start(), calls=%async_computation.6 | async-start | bytes 2228224 | tf_op jit(solution)/shard_map/reduce_scatter | solution.py:37
  347.2 118.8 %copy-start.2 = (f32[256,128]{1,0:T(8,128)S(1)}, f32[256,128]{1,0:T(8,128)}, u32[]{:S(2)}) copy-start(f32[256,128]{1,0:T(8,128)} %reduce-scatter.3.cloned.1.call-done) | copy-start | bytes 393220
  347.2 3.1 copy-start.6
  354.1 3.1 copy-start.6
  360.9 3.1 copy-start.6
  367.8 3.1 copy-start.6
  374.6 3.1 copy-start.6
  381.5 3.1 copy-start.6
  388.3 3.1 copy-start.6
  395.2 3.1 copy-start.6
  402.0 1.4 copy-start
  537.9 0.8 copy-start.4
Sparse Core Ops, SparseCore 0:
  10.9 48.0 all-gather.5
  61.3 53.3 all-gather.3
  171.1 60.3 reduce-scatter.2
  305.7 41.2 all-gather.7
  403.5 62.4 reduce-scatter.4
where the time goes:
time: 546 us; the launch traced here: 545 us
  waiting for transfers between devices  267 us (49%)
  blocking collectives  136 us (25%)
  matrix products  109 us (20%)
  between operations  13.9 us (3%)
  other arithmetic  13.8 us (3%)
    psum x2, blocking collectives, on_device(): lax.psum((jnp.sum(members, axis=0), jnp.sum(members * scores, axis=0)), (...  136 us
    reduce_scatter x2, waiting for transfers between devices, on_device(): lax.psum_scatter(kernel_product(features, column_panel, members_column),...  123 us
    all_gather x2, waiting for transfers between devices, on_device(): members_column = lax.all_gather(members, 'row', axis=0, tiled=True)  88.4 us
    dot_general x16, matrix products, block_product(): jnp.dot(kernel, members, precision=lax.Precision.HIGHEST, preferred_eleme...  58.9 us
    all_gather x1, waiting for transfers between devices, on_device(): column_panel = lax.all_gather(own_rows, 'row', axis=0, tiled=True)  55.7 us
    dot_general x16, matrix products, block_product(): jnp.einsum('bf,nf->bn', block, right_rows, preferred_element_type=jnp.flo...  50 us
  transfers between devices with their start and end apart: 5, of which 5 were waited for; matrix products, arithmetic and copies ran while one was open for 0% of the time, Pallas kernels for 0%

commit v1 on v0

--- a/solution.py
+++ b/solution.py
@@ -41,7 +41,7 @@
             tiled=True,
         )
         cluster_size, weighted = lax.psum(
-            (jnp.sum(members, axis=0), jnp.sum(members * scores, axis=0)), ("row", "col")
+            lax.psum((jnp.sum(members, axis=0), jnp.sum(members * scores, axis=0)), "row"), "col"
         )
         compact = weighted / (cluster_size * cluster_size)
         distance = compact[None, :] - 2.0 * scores / cluster_size[None, :]

time: 546 us -> 516 us (0.945)
  blocking collectives: 136 us -> 109 us
    psum x2 -> x4, blocking collectives: 136 us -> 109 us  [the longest x2 67.8 us: on_device(): lax.psum(lax.psum((jnp.sum(members, axis=0), jnp.sum(members * scores, ax...]
where the time goes in v1:
time: 516 us
  waiting for transfers between devices  264 us (51%)
  matrix products  109 us (21%)
  blocking collectives  109 us (21%)
  between operations  13.9 us (3%)
  other arithmetic  13.8 us (3%)
    reduce_scatter x2, waiting for transfers between devices, on_device(): lax.psum_scatter(kernel_product(features, column_panel, members_column),...  123 us
    all_gather x2, waiting for transfers between devices, on_device(): members_column = lax.all_gather(members, 'row', axis=0, tiled=True)  85.5 us
    psum x2, blocking collectives, on_device(): lax.psum(lax.psum((jnp.sum(members, axis=0), jnp.sum(members * scores, ax...  67.8 us
    dot_general x16, matrix products, block_product(): jnp.dot(kernel, members, precision=lax.Precision.HIGHEST, preferred_eleme...  58.9 us
    all_gather x1, waiting for transfers between devices, on_device(): column_panel = lax.all_gather(own_rows, 'row', axis=0, tiled=True)  55.7 us
    dot_general x16, matrix products, block_product(): jnp.einsum('bf,nf->bn', block, right_rows, preferred_element_type=jnp.flo...  50 us
    psum x2, blocking collectives, on_device(): lax.psum((jnp.sum(members, axis=0), jnp.sum(members * scores, axis=0)), '...  41.3 us
  transfers between devices with their start and end apart: 5, of which 5 were waited for; matrix products, arithmetic and copies ran while one was open for 0% of the time, Pallas kernels for 0%

profile of v1, /device:TPU:1, one launch (start us, length us, event | category | flops | bytes accessed | tf_op | source)
XLA Modules:
  0.0 515.6 jit_solution(3784074950429509640)
XLA Ops:
  8.2 1.7 exponential_divide_fusion
  10.0 1.7 constant_dynamic-slice_fusion
  11.7 47.2 %all-gather.6.cloned.1.call-done = f32[2048,128]{1,0:T(8,128)} async-done(((f32[256,128]{1,0:T(8,128)}), f32[2048,128]{1,0:T(8,128)}) %all-gather.6.cloned.1.call-update) | async-done | bytes 1048592 | tf_op jit(solution)/shard_map/all_gather | solution.py:36
  59.0 55.7 %all-gather.4.cloned.1.call-done = bf16[2048,512]{1,0:T(8,128)(2,1)} async-done(((bf16[256,512]{1,0:T(8,128)(2,1)}), bf16[2048,512]{1,0:T(8,128)(2,1)}) %all-gather.4.cloned.1.call-update) | async-done | bytes 2097168 | tf_op jit(solution)/shard_map/all_gather | solution.py:31
  114.8 54.8 %while.20 = (s32[]{:T(128)}, f32[8,512,128]{2,1,0:T(8,128)S(1)}, bf16[8,512,512]{2,1,0:T(8,128)(2,1)}, bf16[2048,512]{1,0:T(8,128)(2,1)}, f32[2048,128]{1,0:T(8,128)}, /*index=5*/s32[]{:T(128)}) while((s32[]{:T(128)}, f32[8,512,128]{2,1,0:T(8,128)S(1)}, bf16[8,512,512]{2,1,0:T(8,128)(2,1)}, bf16[2048,512]{1,0:T(8,128)(2,1)}, ...), condition=%wide.region_2.3_spmd, body=%wide.region_1.2_spmd.sunk | while | flops 2688548864 | bytes 16515685 | solution.py:24
  114.9 3.1 fusion.48
  118.0 3.7 fusion.49
  121.7 3.1 fusion.48
  124.9 3.7 fusion.49
  128.6 3.1 fusion.48
  131.7 3.7 fusion.49
  135.4 3.1 fusion.48
  138.6 3.7 fusion.49
  142.3 3.1 fusion.48
  145.4 3.7 fusion.49
  149.1 3.1 fusion.48
  152.3 3.7 fusion.49
  156.0 3.1 fusion.48
  159.1 3.7 fusion.49
  162.8 3.1 fusion.48
  166.0 3.7 fusion.49
  169.7 1.3 copy-done.1
  171.0 60.5 %reduce-scatter.3.cloned.1.call-done = f32[256,128]{1,0:T(8,128)} async-done(((f32[4096,128]{1,0:T(8,128)}), f32[256,128]{1,0:T(8,128)}) %reduce-scatter.3.cloned.1.call-update) | async-done | bytes 131088 | tf_op jit(solution)/shard_map/reduce_scatter | solution.py:37
  232.6 20.9 %all-reduce.3 = (f32[128]{0:T(128)S(1)}, f32[128]{0:T(128)S(1)}) all-reduce(f32[128]{0:T(128)S(1)} %get-tuple-element.61, f32[128]{0:T(128)S(1)} %get-tuple-element.60), channel_id=1, replica_groups=mesh['row'=8,'col'=16] {'row'}, use_global_device_ids=true, to_apply=%region_8.9 | all-reduce | flops 256 | bytes 2048 | tf_op jit(solution)/shard_map/psum | solution.py:44
  253.5 33.6 %all-reduce.1 = (f32[128]{0:T(128)S(1)}, f32[128]{0:T(128)S(1)}) all-reduce(f32[128]{0:T(128)S(1)} %get-tuple-element.88, f32[128]{0:T(128)S(1)} %get-tuple-element.89), channel_id=1, replica_groups=mesh['row'=8,'col'=16] {'col'}, use_global_device_ids=true, to_apply=%region_9.10 | all-reduce | flops 256 | bytes 2048 | tf_op jit(solution)/shard_map/psum | solution.py:43
  290.4 1.7 broadcast_divide_fusion
  292.2 38.3 %all-gather.8.cloned.1.call-done = f32[2048,128]{1,0:T(8,128)} async-done(((f32[256,128]{1,0:T(8,128)}), f32[2048,128]{1,0:T(8,128)}) %all-gather.8.cloned.1.call-update) | async-done | bytes 1048592 | tf_op jit(solution)/shard_map/all_gather | solution.py:36
  330.6 54.8 %while.21 = (s32[]{:T(128)}, f32[8,512,128]{2,1,0:T(8,128)S(1)}, bf16[8,512,512]{2,1,0:T(8,128)(2,1)}, bf16[2048,512]{1,0:T(8,128)(2,1)}, f32[2048,128]{1,0:T(8,128)}, /*index=5*/s32[]{:T(128)}) while((s32[]{:T(128)}, f32[8,512,128]{2,1,0:T(8,128)S(1)}, bf16[8,512,512]{2,1,0:T(8,128)(2,1)}, bf16[2048,512]{1,0:T(8,128)(2,1)}, ...), condition=%wide.region_14.15_spmd, body=%wide.region_13.14_spmd.sunk | while | flops 2688548864 | bytes 16515685 | solution.py:24
  330.7 3.1 fusion.53
  333.8 3.7 fusion.54
  337.5 3.1 fusion.53
  340.7 3.7 fusion.54
  344.4 3.1 fusion.53
  347.5 3.7 fusion.54
  351.2 3.1 fusion.53
  354.4 3.7 fusion.54
  358.1 3.1 fusion.53
  361.2 3.7 fusion.54
  364.9 3.1 fusion.53
  368.1 3.7 fusion.54
  371.8 3.1 fusion.53
  374.9 3.7 fusion.54
  378.6 3.1 fusion.53
  381.8 3.7 fusion.54
  385.5 1.3 copy-done
  386.9 62.5 %reduce-scatter.5.cloned.1.call-done = f32[256,128]{1,0:T(8,128)} async-done(((f32[4096,128]{1,0:T(8,128)}), f32[256,128]{1,0:T(8,128)}) %reduce-scatter.5.cloned.1.call-update) | async-done | bytes 131088 | tf_op jit(solution)/shard_map/reduce_scatter | solution.py:37
  450.4 20.4 %all-reduce.2 = (f32[128]{0:T(128)S(1)}, f32[128]{0:T(128)S(1)}) all-reduce(f32[128]{0:T(128)S(1)} %get-tuple-element.59, f32[128]{0:T(128)S(1)} %get-tuple-element.58), channel_id=1, replica_groups=mesh['row'=8,'col'=16] {'row'}, use_global_device_ids=true, to_apply=%region_20.21 | all-reduce | flops 256 | bytes 2048 | tf_op jit(solution)/shard_map/psum | solution.py:44
  470.8 34.2 %all-reduce = (f32[128]{0:T(128)S(1)}, f32[128]{0:T(128)S(1)}) all-reduce(f32[128]{0:T(128)S(1)} %get-tuple-element.86, f32[128]{0:T(128)S(1)} %get-tuple-element.87), channel_id=1, replica_groups=mesh['row'=8,'col'=16] {'col'}, use_global_device_ids=true, to_apply=%region_21.22 | all-reduce | flops 256 | bytes 2048 | tf_op jit(solution)/shard_map/psum | solution.py:43
  (68 shorter events, 11.1 us)
Async XLA Ops:
  7.2 51.8 %all-gather.6.cloned.1.call-start = ((), (), s32[]{:S(2)}) async-start(), calls=%async_computation.3 | async-start | bytes 1179648 | tf_op jit(solution)/shard_map/all_gather | solution.py:36
  9.9 104.8 %all-gather.4.cloned.1.call-start = ((), (), s32[]{:S(2)}) async-start(), calls=%async_computation.2 | async-start | bytes 2359296 | tf_op jit(solution)/shard_map/all_gather | solution.py:31
  11.7 219.8 %reduce-scatter.3.cloned.1.call-start = ((), (), s32[]{:S(2)}) async-start(), calls=%async_computation.4 | async-start | bytes 2228224 | tf_op jit(solution)/shard_map/reduce_scatter | solution.py:37
  114.8 116.7 %copy-start.3 = (f32[256,128]{1,0:T(8,128)S(1)}, f32[256,128]{1,0:T(8,128)}, u32[]{:S(2)}) copy-start(f32[256,128]{1,0:T(8,128)} %param.7) | copy-start | bytes 393220
  114.8 3.1 copy-start.5
  121.7 3.1 copy-start.5
  128.6 3.1 copy-start.5
  135.4 3.1 copy-start.5
  142.3 3.1 copy-start.5
  149.1 3.1 copy-start.5
  156.0 3.1 copy-start.5
  162.8 3.1 copy-start.5
  169.7 1.3 copy-start.1
  171.0 159.5 %all-gather.8.cloned.1.call-start = ((), (), s32[]{:S(2)}) async-start(), calls=%async_computation.5 | async-start | bytes 1179648 | tf_op jit(solution)/shard_map/all_gather | solution.py:36
  292.2 157.2 %reduce-scatter.5.cloned.1.call-start = ((), (), s32[]{:S(2)}) async-start(), calls=%async_computation.6 | async-start | bytes 2228224 | tf_op jit(solution)/shard_map/reduce_scatter | solution.py:37
  330.6 118.7 %copy-start.2 = (f32[256,128]{1,0:T(8,128)S(1)}, f32[256,128]{1,0:T(8,128)}, u32[]{:S(2)}) copy-start(f32[256,128]{1,0:T(8,128)} %reduce-scatter.3.cloned.1.call-done) | copy-start | bytes 393220
  330.7 3.1 copy-start.6
  337.5 3.1 copy-start.6
  344.4 3.1 copy-start.6
  351.2 3.1 copy-start.6
  358.1 3.1 copy-start.6
  364.9 3.1 copy-start.6
  371.8 3.1 copy-start.6
  378.6 3.1 copy-start.6
  385.5 1.4 copy-start
  508.2 0.8 copy-start.4
Sparse Core Ops, SparseCore 0:
  10.9 48.0 all-gather.5
  61.3 53.3 all-gather.3
  171.1 60.3 reduce-scatter.2
  292.3 38.1 all-gather.7
  387.0 62.3 reduce-scatter.4
